TPU v7x, 256 devices: a whole 4x4x8 slice. The times are simulated.
256 devices in a mesh: segment: 8 (over z), tile: 32 (over x, y, core).
Axes of the slice: x: 4, y: 4, z: 8, core: 2. Of those that a mesh axis runs over, the one named last changes fastest.
Arguments:
- latent: bfloat16 [4, 8, 128, 384], P(None, None, 'tile'), may hold values from -6 to 6
- frame_order: int32 [4], replicated, may hold values from 0 to 3, each once
- section_weight: bfloat16 [8, 27, 384, 384], P('segment'), may hold values from -0.0625 to 0.0625
- section_gain: bfloat16 [8, 384], P('segment'), may hold values from 0.5 to 1.5
- up_weight: bfloat16 [27, 384, 192], P(None, 'tile'), may hold values from -0.0625 to 0.0625
- reward_weight: bfloat16 [49152, 1280], P(None, 'tile'), may hold values from -0.02734375 to 0.02734375
- reward_coef: float32 [1280], P('tile'), may hold values from -6 to 6
Outputs:
- input_grads: float32 [8, 4, 8, 128, 384], P('segment', None, None, 'tile')
All inputs are finite; a program needn't handle non-finite values.
Results may differ from a plain program's by a relative error of at most 0.03.
Values may be sent and summed in bfloat16 or wider, within the bound.
No kernel may reach another device: no remote copies, remote signals or barrier semaphores. Data moves between devices by JAX's collectives and lax.ppermute only.
A program may use at most 128 MiB of HBM per device.

v0:
```python
import jax
import jax.numpy as jnp
from jax import lax
from jax.sharding import PartitionSpec as P

P_SIZE = 16
EPS = 1e-06


def with_halo(cells, sides, width):
    for axis, dim in sides:
        count = lax.axis_size(axis)
        ends = count - 1
        head = lax.slice_in_dim(cells, 0, width, axis=dim)
        tail = lax.slice_in_dim(cells, cells.shape[dim] - width, cells.shape[dim], axis=dim)
        cells = jnp.concatenate(
            [
                lax.ppermute(tail, axis, [(i, (i + 1) % count) for i in range(ends)]),
                cells,
                lax.ppermute(head, axis, [((i + 1) % count, i) for i in range(ends)]),
            ],
            axis=dim,
        )
    return cells


def from_behind(block, axis, distance):
    devices = range(lax.axis_size(axis))
    route = [(i - distance, i) for i in devices if i - distance in devices]
    return lax.ppermute(block, axis, route)


def section_act(inputs, gain_row):
    as_float = inputs.astype(jnp.float32)
    inv_norm = lax.rsqrt(jnp.mean(as_float * as_float, axis=-1, keepdims=True) + EPS)
    return jax.nn.silu(as_float * inv_norm * gain_row.astype(jnp.float32))


def causal_taps(stacked, height, width):
    pieces = []
    for time_off in range(3):
        for row_off in range(3):
            for col_off in range(3):
                pieces.append(
                    stacked[time_off, row_off : row_off + height, col_off : col_off + width]
                )
    return jnp.stack(pieces, axis=2).reshape(height * width, -1)


def reverse_taps(stacked, height, width):
    pieces = []
    for time_off in range(3):
        for row_off in range(3):
            for col_off in range(3):
                pieces.append(
                    stacked[
                        time_off,
                        2 - row_off : 2 - row_off + height,
                        2 - col_off : 2 - col_off + width,
                    ]
                )
    return jnp.stack(pieces, axis=2).reshape(height * width, -1)


def plane_taps(plane, height, width):
    pieces = []
    for row_off in range(3):
        for col_off in range(3):
            pieces.append(
                plane[2 - row_off : 2 - row_off + height, 2 - col_off : 2 - col_off + width]
            )
    return jnp.stack(pieces, axis=2).reshape(height * width, -1)


def pad_rows(stacked):
    return jnp.pad(stacked, ((0, 0), (1, 1), (0, 0), (0, 0)))


def on_device(
    latent, frame_order, section_weight, section_gain, up_weight, reward_weight, reward_coef
):
    segment_count = lax.axis_size("segment")
    segment_at = lax.axis_index("segment")
    frame_count, height, width_dev, channels = latent.shape
    weight_fwd = section_weight[0].reshape(27 * channels, channels)
    weight_back = section_weight[0].transpose(0, 2, 1).reshape(27 * channels, channels)
    gain_row = section_gain[0]
    is_first = segment_at == 0
    is_last = segment_at == segment_count - 1
    tick_count = frame_count + segment_count - 1
    zero_rim = jnp.zeros((height, width_dev + 2, channels), jnp.bfloat16)
    zero_frames = jnp.zeros((frame_count, height, width_dev, channels), jnp.bfloat16)

    def forward_tick(loop_step, carried):
        prev_two, prev_one, incoming, inputs_kept, outputs_kept = carried
        frame_slot = loop_step - segment_at
        is_live = (frame_slot >= 0) & (frame_slot < frame_count)
        frame_at = jnp.clip(frame_slot, 0, frame_count - 1)
        own_frame = lax.dynamic_index_in_dim(latent, frame_order[frame_at], 0, keepdims=False)
        segment_in = jnp.where(is_first, own_frame, incoming)
        activated = section_act(segment_in, gain_row).astype(jnp.bfloat16)
        act_rim = with_halo(activated, (("tile", 1),), 1)
        window = pad_rows(jnp.stack([prev_two, prev_one, act_rim]))

        def live_conv():
            return jnp.dot(
                causal_taps(window, height, width_dev),
                weight_fwd,
                preferred_element_type=jnp.float32,
            )

        def dead_conv():
            return jnp.zeros((height * width_dev, channels), jnp.float32)

        conv_out = lax.cond(is_live, live_conv, dead_conv)
        segment_out = (
            segment_in.astype(jnp.float32) + conv_out.reshape(height, width_dev, channels)
        ).astype(jnp.bfloat16)
        prev_two = jnp.where(is_live, prev_one, prev_two)
        prev_one = jnp.where(is_live, act_rim, prev_one)
        inputs_kept = jnp.where(is_live, inputs_kept.at[frame_at].set(segment_in), inputs_kept)
        outputs_kept = jnp.where(is_live, outputs_kept.at[frame_at].set(segment_out), outputs_kept)
        incoming = from_behind(segment_out, "segment", 1)
        return (prev_two, prev_one, incoming, inputs_kept, outputs_kept)

    start_fwd = (
        zero_rim,
        zero_rim,
        jnp.zeros((height, width_dev, channels), jnp.bfloat16),
        zero_frames,
        zero_frames,
    )
    carried = lax.fori_loop(0, tick_count, forward_tick, start_fwd)
    inputs_kept = carried[3]
    outputs_kept = carried[4]
    gathered_up = lax.all_gather(up_weight, "tile", axis=1, tiled=True)
    up_width = gathered_up.shape[2]
    up_flat = gathered_up.reshape(27 * channels, up_width)
    back_up = (
        gathered_up.reshape(3, 9, channels, up_width)
        .transpose(1, 3, 0, 2)
        .reshape(9 * up_width, 3 * channels)
    )
    padded_deep = jnp.concatenate(
        [jnp.zeros((2, height, width_dev, channels), jnp.bfloat16), outputs_kept], 0
    )
    collected = jnp.zeros((frame_count + 2, height, width_dev, channels), jnp.float32)
    for frame_slot in range(frame_count):
        head_window = lax.dynamic_slice_in_dim(padded_deep, frame_slot, 3, 0)
        widened = with_halo(
            jnp.repeat(jnp.repeat(head_window, 2, axis=1), 2, axis=2), (("tile", 2),), 1
        )
        preact = jnp.dot(
            causal_taps(pad_rows(widened), 2 * height, 2 * width_dev),
            up_flat,
            preferred_element_type=jnp.float32,
        )
        preact = preact.reshape(2 * height, 2 * width_dev, up_width)
        features = jax.nn.silu(preact).astype(jnp.bfloat16)
        gathered = lax.all_gather(
            features.reshape(2 * height, 2 * width_dev * up_width), "tile", axis=1, tiled=True
        )
        full_width = gathered.shape[1] // up_width
        patches = (
            gathered.reshape(2 * height // P_SIZE, P_SIZE, full_width // P_SIZE, P_SIZE, up_width)
            .transpose(0, 2, 1, 3, 4)
            .reshape(-1, P_SIZE * P_SIZE * up_width)
        )
        logits = jnp.dot(patches, reward_weight, preferred_element_type=jnp.float32)
        squashed = jnp.tanh(logits)
        logit_grad = (reward_coef * (1.0 - squashed * squashed)).astype(jnp.bfloat16)
        patch_grad = lax.dot_general(
            logit_grad, reward_weight, (((1,), (1,)), ((), ())), preferred_element_type=jnp.float32
        )
        patch_back = patch_grad.reshape(
            2 * height // P_SIZE, full_width // P_SIZE, P_SIZE, P_SIZE, up_width
        ).transpose(0, 2, 1, 3, 4)
        patch_back = patch_back.reshape(2 * height, full_width * up_width)
        feat_grad = (
            lax.psum_scatter(
                patch_back.astype(jnp.bfloat16), "tile", scatter_dimension=1, tiled=True
            )
            .astype(jnp.float32)
            .reshape(2 * height, 2 * width_dev, up_width)
        )
        sigmoid_p = jax.nn.sigmoid(preact)
        preact_grad = (feat_grad * sigmoid_p * (1.0 + preact * (1.0 - sigmoid_p))).astype(
            jnp.bfloat16
        )
        grad_rim_up = with_halo(preact_grad, (("tile", 1),), 1)
        grad_pad = jnp.pad(grad_rim_up, ((1, 1), (0, 0), (0, 0)))
        contribution = jnp.dot(
            plane_taps(grad_pad, 2 * height, 2 * width_dev),
            back_up,
            preferred_element_type=jnp.float32,
        )
        contribution = contribution.reshape(height, 2, width_dev, 2, 3, channels).sum(axis=(1, 3))
        frame_map = (
            jnp.arange(frame_count + 2)[None, :] == (frame_slot + jnp.arange(3))[:, None]
        ).astype(jnp.float32)
        produced = jnp.einsum("dk,hwdc->khwc", frame_map, contribution)
        collected = collected + jnp.where(is_last, produced, 0.0)
    deep_grad = collected[2:]

    def backward_tick(loop_step, carried):
        next_one, next_two, incoming, grads_kept = carried
        frame_slot = loop_step - (segment_count - 1 - segment_at)
        is_live = (frame_slot >= 0) & (frame_slot < frame_count)
        frame_at = frame_count - 1 - jnp.clip(frame_slot, 0, frame_count - 1)
        own_grad = lax.dynamic_index_in_dim(deep_grad, frame_at, 0, keepdims=False)
        grad_out = jnp.where(is_last, own_grad, incoming)
        grad_rim = with_halo(grad_out.astype(jnp.bfloat16), (("tile", 1),), 1)
        window = pad_rows(jnp.stack([next_two, next_one, grad_rim]))
        segment_in = lax.dynamic_index_in_dim(inputs_kept, frame_at, 0, keepdims=False)

        def live_back():
            conv_back = jnp.dot(
                reverse_taps(window, height, width_dev),
                weight_back,
                preferred_element_type=jnp.float32,
            )
            _, pullback = jax.vjp(
                lambda values: section_act(values, gain_row), segment_in.astype(jnp.float32)
            )
            return pullback(conv_back.reshape(height, width_dev, channels))[0]

        def dead_back():
            return jnp.zeros((height, width_dev, channels), jnp.float32)

        grad_in = grad_out + lax.cond(is_live, live_back, dead_back)
        next_two = jnp.where(is_live, next_one, next_two)
        next_one = jnp.where(is_live, grad_rim, next_one)
        grads_kept = jnp.where(is_live, grads_kept.at[frame_at].set(grad_in), grads_kept)
        incoming = from_behind(grad_in.astype(jnp.bfloat16), "segment", -1).astype(grad_in.dtype)
        return (next_one, next_two, incoming, grads_kept)

    start_bwd = (
        zero_rim,
        zero_rim,
        jnp.zeros((height, width_dev, channels), jnp.float32),
        jnp.zeros((frame_count, height, width_dev, channels), jnp.float32),
    )
    carried = lax.fori_loop(0, tick_count, backward_tick, start_bwd)
    return carried[3][None]


def solution(mesh):
    in_specs = (
        P(None, None, "tile", None),
        P(),
        P("segment", None, None, None),
        P("segment", None),
        P(None, "tile", None),
        P(None, "tile"),
        P("tile"),
    )
    out_specs = P("segment", None, None, "tile", None)
    return jax.shard_map(
        on_device, mesh=mesh, in_specs=in_specs, out_specs=out_specs, check_vma=False
    )
```

profile of v0, /device:TPU:2, one launch (start us, length us, event | category | flops | bytes accessed | tf_op | source)
XLA Modules:
  0.0 1193.0 jit_solution(10508438219004715807)
XLA Ops:
  7.3 270.5 %while.49 = (s32[]{:T(128)}, bf16[8,6,384]{2,0,1:T(8,128)(2,1)S(1)}, bf16[8,6,384]{2,0,1:T(8,128)(2,1)S(1)}, bf16[8,4,384]{2,0,1:T(8,128)(2,1)S(1)}, bf16[4,8,4,...) while((s32[]{:T(128)}, ...), condition=%wide.region_5.6_spmd.clone, body=%wide.region_0.5_spmd.clone.sunk | while | flops 255259072 | bytes 13963990 | solution.py:133
  19.4 5.1 collective-permute-done.1
  24.5 5.1 conditional.6
  47.8 5.1 conditional.6
  74.0 5.1 conditional.6
  100.2 5.1 conditional.6
  127.0 9.3 collective-permute-start.2
  174.4 7.0 collective-permute-start.2
  219.4 7.1 collective-permute-start.2
  243.4 5.4 collective-permute-start.2
  265.8 10.5 collective-permute-start.2
  281.3 5.8 collective-permute-start.11
  290.1 5.8 collective-permute-start.7
  303.7 5.8 collective-permute-start.15
  314.7 5.9 collective-permute-start.19
  336.4 25.2 %all-gather.6.cloned.1.call-done = bf16[27,384,192]{2,0,1:T(8,128)(2,1)} async-done(((bf16[27,12,192]{2,0,1:T(8,128)(2,1)}), bf16[27,384,192]{2,0,1:T(8,128)(2,1)}) %all-gather.6.cloned.1.call-update) | async-done | bytes 3981328 | tf_op jit(solution)/shard_map/all_gather | solution.py:136
  361.6 10.1 multiply_convert_fusion.7
  382.8 10.1 multiply_convert_fusion.5
  404.0 9.5 multiply_convert_fusion.3
  423.9 9.4 multiply_convert_fusion.1
  443.2 7.4 convolution_convert_fusion.3
  460.7 9.4 all-gather.10.cloned.1.call-done
  478.9 7.3 convolution_convert_fusion.2
  496.2 23.6 %all-gather.12.cloned.1.call-done = bf16[16,49152]{1,0:T(8,128)(2,1)} async-done(((bf16[16,1536]{1,0:T(8,128)(2,1)}), bf16[16,49152]{1,0:T(8,128)(2,1)}) %all-gather.12.cloned.1.call-update) | async-done | bytes 1572880 | tf_op jit(solution)/shard_map/all_gather | solution.py:160
  528.7 7.3 convolution_convert_fusion.1
  546.2 23.4 %all-gather.14.cloned.1.call-done = bf16[16,49152]{1,0:T(8,128)(2,1)} async-done(((bf16[16,1536]{1,0:T(8,128)(2,1)}), bf16[16,49152]{1,0:T(8,128)(2,1)}) %all-gather.14.cloned.1.call-update) | async-done | bytes 1572880 | tf_op jit(solution)/shard_map/all_gather | solution.py:160
  578.5 7.3 convolution_convert_fusion
  595.6 11.7 copy.635
  607.3 8.6 copy.533
  615.8 5.5 copy.534
  624.1 6.6 copy.535
  630.7 28.2 %reduce-scatter.5.cloned.1.call-done = bf16[16,1536]{1,0:T(8,128)(2,1)} async-done(((bf16[16,49152]{1,0:T(8,128)(2,1)}), bf16[16,1536]{1,0:T(8,128)(2,1)}) %reduce-scatter.5.cloned.1.call-update) | async-done | bytes 49168 | tf_op jit(solution)/shard_map/reduce_scatter | solution.py:180
  661.8 5.8 collective-permute-start.9
  667.6 80.6 %reduce-scatter.7.cloned.1.call-done = bf16[16,1536]{1,0:T(8,128)(2,1)} async-done(((bf16[16,49152]{1,0:T(8,128)(2,1)}), bf16[16,1536]{1,0:T(8,128)(2,1)}) %reduce-scatter.7.cloned.1.call-update) | async-done | bytes 49168 | tf_op jit(solution)/shard_map/reduce_scatter | solution.py:180
  751.2 5.8 collective-permute-start.13
  756.9 80.6 %reduce-scatter.9.cloned.1.call-done = bf16[16,1536]{1,0:T(8,128)(2,1)} async-done(((bf16[16,49152]{1,0:T(8,128)(2,1)}), bf16[16,1536]{1,0:T(8,128)(2,1)}) %reduce-scatter.9.cloned.1.call-update) | async-done | bytes 49168 | tf_op jit(solution)/shard_map/reduce_scatter | solution.py:180
  838.6 88.3 %reduce-scatter.11.cloned.1.call-done = bf16[16,1536]{1,0:T(8,128)(2,1)} async-done(((bf16[16,49152]{1,0:T(8,128)(2,1)}), bf16[16,1536]{1,0:T(8,128)(2,1)}) %reduce-scatter.11.cloned.1.call-update) | async-done | bytes 49168 | tf_op jit(solution)/shard_map/reduce_scatter | solution.py:180
  929.9 5.8 collective-permute-start.17
  939.1 5.8 collective-permute-start.21
  964.4 221.2 %while.50 = (s32[]{:T(128)}, bf16[8,6,384]{2,0,1:T(8,128)(2,1)S(1)}, bf16[8,6,384]{2,0,1:T(8,128)(2,1)S(1)}, f32[8,4,384]{2,0,1:T(8,128)S(1)}, f32[4,8,4,384]{3,...) while((s32[]{:T(128)}, ...), condition=%wide.region_20.21_spmd.clone, body=%wide.region_14.20_spmd.clone.sunk | while | flops 255418992 | bytes 14603769 | solution.py:243
  1067.3 33.6 %collective-permute-done.5 = bf16[8,4,384]{2,0,1:T(8,128)(2,1)S(1)} collective-permute-done((bf16[8,4,384]{2,0,1:T(8,128)(2,1)S(1)}, bf16[8,4,384]{2,0,1:T(8,128)(2,1)S(1)}, u32[]{:S(2)}, u32[]{:S(2)}) %collective-permute-start.5) | collective-permute-done | bytes 24608 | tf_op jit(solution)/shard_map/while/body/eval_jaxpr/ppermute | solution.py:30
  1110.1 5.4 conditional.7
  1117.5 4.9 collective-permute-done.5
  1131.5 5.4 conditional.7
  1139.0 4.9 collective-permute-done.5
  1153.0 5.4 conditional.7
  1160.4 4.9 collective-permute-done.5
  1174.5 5.4 conditional.7
  (997 shorter events, 557.9 us)
Async XLA Ops:
  6.5 355.1 %all-gather.6.cloned.1.call-start = ((), (), s32[]{:S(2)}) async-start(), calls=%async_computation.4 | async-start | bytes 6488064 | tf_op jit(solution)/shard_map/all_gather | solution.py:136
  40.7 7.1 collective-permute-start.1
  66.9 7.1 collective-permute-start.1
  93.1 7.1 collective-permute-start.1
  127.0 10.8 collective-permute-start.2
  145.5 7.1 collective-permute-start.1
  166.6 7.1 collective-permute-start.1
  174.4 8.5 collective-permute-start.2
  190.5 7.1 collective-permute-start.1
  211.7 7.1 collective-permute-start.1
  219.4 8.6 collective-permute-start.2
  235.7 7.1 collective-permute-start.1
  258.1 7.1 collective-permute-start.1
  265.8 12.0 %collective-permute-start.2 = (bf16[8,4,384]{2,0,1:T(8,128)(2,1)S(1)}, bf16[8,4,384]{2,0,1:T(8,128)(2,1)S(1)}, u32[]{:S(2)}, u32[]{:S(2)}) collective-permute-start(bf16[8,4,384]{2,0,1:T(8,128)(2,1)S(1)} %get-tuple-element.1160), channel_id=1, source_target_pairs={{0,32},{32,64},{64,96},{96,128},{128,160},{160,192},{192,224},{1,3... | collective-permute-start | bytes 73736 | tf_op jit(solution)/shard_map/while/body/eval_jaxpr/ppermute | solution.py:30
  279.4 24.3 %collective-permute-start.10 = (bf16[3,16,1,384]{3,2,1,0:T(2,128)(2,1)}, bf16[3,16,1,384]{3,2,1,0:T(2,128)(2,1)S(1)}, u32[]{:S(2)}, u32[]{:S(2)}) collective-permute-start(bf16[3,16,1,384]{3,2,1,0:T(2,128)(2,1)} %get-tuple-element.963), channel_id=1, source_target_pairs={{0,1},{1,2},{2,3},{3,4},{4,5},{5,6},{6,7},{7,8},{8,9},{9,10},{10,1... | collective-permute-start | bytes 110600 | tf_op jit(solution)/shard_map/ppermute | solution.py:18
  281.3 28.2 %collective-permute-start.11 = (bf16[3,16,1,384]{3,2,1,0:T(2,128)(2,1)}, bf16[3,16,1,384]{3,2,1,0:T(2,128)(2,1)}, u32[]{:S(2)}, u32[]{:S(2)}) collective-permute-start(bf16[3,16,1,384]{3,2,1,0:T(2,128)(2,1)} %get-tuple-element.964), channel_id=1, source_target_pairs={{1,0},{2,1},{3,2},{4,3},{5,4},{6,5},{7,6},{8,7},{9,8},{10,9},{11,1... | collective-permute-start | bytes 110600 | tf_op jit(solution)/shard_map/ppermute | solution.py:20
  288.2 26.5 %collective-permute-start.6 = (bf16[3,16,1,384]{3,2,1,0:T(2,128)(2,1)}, bf16[3,16,1,384]{3,2,1,0:T(2,128)(2,1)S(1)}, u32[]{:S(2)}, u32[]{:S(2)}) collective-permute-start(bf16[3,16,1,384]{3,2,1,0:T(2,128)(2,1)} %get-tuple-element.961), channel_id=1, source_target_pairs={{0,1},{1,2},{2,3},{3,4},{4,5},{5,6},{6,7},{7,8},{8,9},{9,10},{10,1... | collective-permute-start | bytes 110600 | tf_op jit(solution)/shard_map/ppermute | solution.py:18
  290.1 30.6 %collective-permute-start.7 = (bf16[3,16,1,384]{3,2,1,0:T(2,128)(2,1)}, bf16[3,16,1,384]{3,2,1,0:T(2,128)(2,1)S(1)}, u32[]{:S(2)}, u32[]{:S(2)}) collective-permute-start(bf16[3,16,1,384]{3,2,1,0:T(2,128)(2,1)} %get-tuple-element.962), channel_id=1, source_target_pairs={{1,0},{2,1},{3,2},{4,3},{5,4},{6,5},{7,6},{8,7},{9,8},{10,9},{11,1... | collective-permute-start | bytes 110600 | tf_op jit(solution)/shard_map/ppermute | solution.py:20
  295.9 138.5 %all-gather.8.cloned.1.call-start = ((), (), s32[]{:S(2)}) async-start(), calls=%async_computation.5 | async-start | bytes 1622016 | tf_op jit(solution)/shard_map/all_gather | solution.py:160
  301.7 21.4 %collective-permute-start.14 = (bf16[3,16,1,384]{3,2,1,0:T(2,128)(2,1)}, bf16[3,16,1,384]{3,2,1,0:T(2,128)(2,1)S(1)}, u32[]{:S(2)}, u32[]{:S(2)}) collective-permute-start(bf16[3,16,1,384]{3,2,1,0:T(2,128)(2,1)} %get-tuple-element.965), channel_id=1, source_target_pairs={{0,1},{1,2},{2,3},{3,4},{4,5},{5,6},{6,7},{7,8},{8,9},{9,10},{10,1... | collective-permute-start | bytes 110600 | tf_op jit(solution)/shard_map/ppermute | solution.py:18
  303.7 18.5 %collective-permute-start.15 = (bf16[3,16,1,384]{3,2,1,0:T(2,128)(2,1)}, bf16[3,16,1,384]{3,2,1,0:T(2,128)(2,1)S(1)}, u32[]{:S(2)}, u32[]{:S(2)}) collective-permute-start(bf16[3,16,1,384]{3,2,1,0:T(2,128)(2,1)} %get-tuple-element.966), channel_id=1, source_target_pairs={{1,0},{2,1},{3,2},{4,3},{5,4},{6,5},{7,6},{8,7},{9,8},{10,9},{11,1... | collective-permute-start | bytes 110600 | tf_op jit(solution)/shard_map/ppermute | solution.py:20
  312.8 14.3 %collective-permute-start.18 = (bf16[3,16,1,384]{3,2,1,0:T(2,128)(2,1)}, bf16[3,16,1,384]{3,2,1,0:T(2,128)(2,1)S(1)}, u32[]{:S(2)}, u32[]{:S(2)}) collective-permute-start(bf16[3,16,1,384]{3,2,1,0:T(2,128)(2,1)} %get-tuple-element.967), channel_id=1, source_target_pairs={{0,1},{1,2},{2,3},{3,4},{4,5},{5,6},{6,7},{7,8},{8,9},{9,10},{10,1... | collective-permute-start | bytes 110600 | tf_op jit(solution)/shard_map/ppermute | solution.py:18
  314.7 11.7 collective-permute-start.19
  372.4 97.6 %all-gather.10.cloned.1.call-start = ((), (), s32[]{:S(2)}) async-start(), calls=%async_computation.7 | async-start | bytes 1622016 | tf_op jit(solution)/shard_map/all_gather | solution.py:160
  393.6 126.2 %all-gather.12.cloned.1.call-start = ((), (), s32[]{:S(2)}) async-start(), calls=%async_computation.9 | async-start | bytes 1622016 | tf_op jit(solution)/shard_map/all_gather | solution.py:160
  414.3 155.4 %all-gather.14.cloned.1.call-start = ((), (), s32[]{:S(2)}) async-start(), calls=%async_computation.11 | async-start | bytes 1622016 | tf_op jit(solution)/shard_map/all_gather | solution.py:160
  434.1 224.8 %reduce-scatter.5.cloned.1.call-start = ((), (), s32[]{:S(2)}) async-start(), calls=%async_computation.6 | async-start | bytes 1622016 | tf_op jit(solution)/shard_map/reduce_scatter | solution.py:180
  460.4 287.8 %reduce-scatter.7.cloned.1.call-start = ((), (), s32[]{:S(2)}) async-start(), calls=%async_computation.8 | async-start | bytes 1622016 | tf_op jit(solution)/shard_map/reduce_scatter | solution.py:180
  495.9 341.6 %reduce-scatter.9.cloned.1.call-start = ((), (), s32[]{:S(2)}) async-start(), calls=%async_computation.10 | async-start | bytes 1622016 | tf_op jit(solution)/shard_map/reduce_scatter | solution.py:180
  545.7 381.2 %reduce-scatter.11.cloned.1.call-start = ((), (), s32[]{:S(2)}) async-start(), calls=%async_computation.12 | async-start | bytes 1622016 | tf_op jit(solution)/shard_map/reduce_scatter | solution.py:180
  659.9 270.0 %collective-permute-start.8 = (bf16[16,1,192]{2,1,0:T(2,128)(2,1)S(1)}, bf16[16,1,192]{2,1,0:T(2,128)(2,1)S(1)}, u32[]{:S(2)}, u32[]{:S(2)}) collective-permute-start(bf16[16,1,192]{2,1,0:T(2,128)(2,1)S(1)} %get-tuple-element.985), channel_id=1, source_target_pairs={{0,1},{1,2},{2,3},{3,4},{4,5},{5,6},{6,7},{7,8},{8,9},{9,10},{10,1... | collective-permute-start | bytes 18440 | tf_op jit(solution)/shard_map/ppermute | solution.py:18
  661.8 273.8 %collective-permute-start.9 = (bf16[16,1,192]{2,1,0:T(2,128)(2,1)S(1)}, bf16[16,1,192]{2,1,0:T(2,128)(2,1)S(1)}, u32[]{:S(2)}, u32[]{:S(2)}) collective-permute-start(bf16[16,1,192]{2,1,0:T(2,128)(2,1)S(1)} %get-tuple-element.986), channel_id=1, source_target_pairs={{1,0},{2,1},{3,2},{4,3},{5,4},{6,5},{7,6},{8,7},{9,8},{10,9},{11,1... | collective-permute-start | bytes 18440 | tf_op jit(solution)/shard_map/ppermute | solution.py:20
  749.2 189.8 %collective-permute-start.12 = (bf16[16,1,192]{2,1,0:T(2,128)(2,1)S(1)}, bf16[16,1,192]{2,1,0:T(2,128)(2,1)S(1)}, u32[]{:S(2)}, u32[]{:S(2)}) collective-permute-start(bf16[16,1,192]{2,1,0:T(2,128)(2,1)S(1)} %get-tuple-element.987), channel_id=1, source_target_pairs={{0,1},{1,2},{2,3},{3,4},{4,5},{5,6},{6,7},{7,8},{8,9},{9,10},{10,1... | collective-permute-start | bytes 18440 | tf_op jit(solution)/shard_map/ppermute | solution.py:18
  751.2 193.7 %collective-permute-start.13 = (bf16[16,1,192]{2,1,0:T(2,128)(2,1)S(1)}, bf16[16,1,192]{2,1,0:T(2,128)(2,1)S(1)}, u32[]{:S(2)}, u32[]{:S(2)}) collective-permute-start(bf16[16,1,192]{2,1,0:T(2,128)(2,1)S(1)} %get-tuple-element.988), channel_id=1, source_target_pairs={{1,0},{2,1},{3,2},{4,3},{5,4},{6,5},{7,6},{8,7},{9,8},{10,9},{11,1... | collective-permute-start | bytes 18440 | tf_op jit(solution)/shard_map/ppermute | solution.py:20
  927.9 24.2 %collective-permute-start.16 = (bf16[16,1,192]{2,1,0:T(2,128)(2,1)S(1)}, bf16[16,1,192]{2,1,0:T(2,128)(2,1)S(1)}, u32[]{:S(2)}, u32[]{:S(2)}) collective-permute-start(bf16[16,1,192]{2,1,0:T(2,128)(2,1)S(1)} %get-tuple-element.989), channel_id=1, source_target_pairs={{0,1},{1,2},{2,3},{3,4},{4,5},{5,6},{6,7},{7,8},{8,9},{9,10},{10,1... | collective-permute-start | bytes 18440 | tf_op jit(solution)/shard_map/ppermute | solution.py:18
  929.9 22.2 %collective-permute-start.17 = (bf16[16,1,192]{2,1,0:T(2,128)(2,1)S(1)}, bf16[16,1,192]{2,1,0:T(2,128)(2,1)S(1)}, u32[]{:S(2)}, u32[]{:S(2)}) collective-permute-start(bf16[16,1,192]{2,1,0:T(2,128)(2,1)S(1)} %get-tuple-element.990), channel_id=1, source_target_pairs={{1,0},{2,1},{3,2},{4,3},{5,4},{6,5},{7,6},{8,7},{9,8},{10,9},{11,1... | collective-permute-start | bytes 18440 | tf_op jit(solution)/shard_map/ppermute | solution.py:20
  937.1 20.6 %collective-permute-start.20 = (bf16[16,1,192]{2,1,0:T(2,128)(2,1)S(1)}, bf16[16,1,192]{2,1,0:T(2,128)(2,1)S(1)}, u32[]{:S(2)}, u32[]{:S(2)}) collective-permute-start(bf16[16,1,192]{2,1,0:T(2,128)(2,1)S(1)} %get-tuple-element.991), channel_id=1, source_target_pairs={{0,1},{1,2},{2,3},{3,4},{4,5},{5,6},{6,7},{7,8},{8,9},{9,10},{10,1... | collective-permute-start | bytes 18440 | tf_op jit(solution)/shard_map/ppermute | solution.py:18
  939.1 18.7 %collective-permute-start.21 = (bf16[16,1,192]{2,1,0:T(2,128)(2,1)S(1)}, bf16[16,1,192]{2,1,0:T(2,128)(2,1)S(1)}, u32[]{:S(2)}, u32[]{:S(2)}) collective-permute-start(bf16[16,1,192]{2,1,0:T(2,128)(2,1)S(1)} %get-tuple-element.992), channel_id=1, source_target_pairs={{1,0},{2,1},{3,2},{4,3},{5,4},{6,5},{7,6},{8,7},{9,8},{10,9},{11,1... | collective-permute-start | bytes 18440 | tf_op jit(solution)/shard_map/ppermute | solution.py:20
  966.4 7.1 collective-permute-start.4
  981.3 7.1 collective-permute-start.4
  996.2 7.1 collective-permute-start.4
  1011.1 7.1 collective-permute-start.4
  1042.0 7.1 collective-permute-start.4
  1058.1 7.1 collective-permute-start.4
  1065.3 35.6 %collective-permute-start.5 = (bf16[8,4,384]{2,0,1:T(8,128)(2,1)S(1)}, bf16[8,4,384]{2,0,1:T(8,128)(2,1)S(1)}, u32[]{:S(2)}, u32[]{:S(2)}) collective-permute-start(bf16[8,4,384]{2,0,1:T(8,128)(2,1)S(1)} %add_convert_fusion.2), channel_id=1, source_target_pairs={{32,0},{64,32},{96,64},{128,96},{160,128},{192,160},{224,192},{33,... | collective-permute-start | bytes 73736 | tf_op jit(solution)/shard_map/while/body/eval_jaxpr/ppermute | solution.py:30
  1102.9 7.1 collective-permute-start.4
  1124.4 7.1 collective-permute-start.4
  1145.9 7.1 collective-permute-start.4
  (61 other events, 456.1 us)
Sparse Core Ops, SparseCore 0:
  296.0 65.5 all-gather.5
  372.5 47.4 all-gather.7
  422.6 47.3 all-gather.9
  472.5 47.3 all-gather.11
  522.3 47.3 all-gather.13
  573.4 85.4 reduce-scatter.4
  662.7 85.4 reduce-scatter.6
  752.0 85.4 reduce-scatter.8
  841.4 85.4 reduce-scatter.10
where the time goes:
time: 1200 us; the launch traced here: 1190 us
  waiting for transfers between devices  546 us (46%)
  starting transfers between devices  237 us (20%)
  local copies, waits for them, and re-layouts  199 us (17%)
  matrix products  119 us (10%)
  other arithmetic  55.6 us (5%)
  loops' own time  21.8 us (2%)
  between operations  15 us (1%)
    reduce_scatter x4, waiting for transfers between devices, on_device(): lax.psum_scatter(patch_back.astype(jnp.bfloat16), 'tile', scatter_dimensi...  278 us
    ppermute x30, waiting for transfers between devices, with_halo(): lax.ppermute(tail, axis, [(i, (i + 1) % count) for i in range(ends)])  93.7 us
    ppermute x22, waiting for transfers between devices, from_behind(): return lax.ppermute(block, axis, route)  92.9 us
    ppermute x30, starting transfers between devices, with_halo(): lax.ppermute(head, axis, [((i + 1) % count, i) for i in range(ends)])  90.8 us
    ppermute x22, starting transfers between devices, from_behind(): return lax.ppermute(block, axis, route)  75.7 us
    ppermute x30, starting transfers between devices, with_halo(): lax.ppermute(tail, axis, [(i, (i + 1) % count) for i in range(ends)])  67.8 us
    all_gather x4, waiting for transfers between devices, on_device(): lax.all_gather(features.reshape(2 * height, 2 * width_dev * up_width), 't...  56.4 us
    unnamed x151, local copies, waits for them, and re-layouts  44.1 us
  transfers between devices with their start and end apart: 91, of which 52 were waited for; matrix products, arithmetic and copies ran while one was open for 21% of the time, Pallas kernels for 0%

commit v1 on v0

--- a/solution.py
+++ b/solution.py
@@ -157,8 +157,16 @@
         )
         preact = preact.reshape(2 * height, 2 * width_dev, up_width)
         features = jax.nn.silu(preact).astype(jnp.bfloat16)
-        gathered = lax.all_gather(
-            features.reshape(2 * height, 2 * width_dev * up_width), "tile", axis=1, tiled=True
+        gathered = jnp.concatenate(
+            lax.all_to_all(
+                jnp.stack(
+                    [features.reshape(2 * height, 2 * width_dev * up_width)] * lax.axis_size("tile")
+                ),
+                "tile",
+                0,
+                0,
+            ),
+            axis=1,
         )
         full_width = gathered.shape[1] // up_width
         patches = (

time: 1200 us -> 1080 us (0.900)
  waiting for transfers between devices: 546 us -> 339 us
  blocking collectives: 0 us -> 28.4 us
  local copies, waits for them, and re-layouts: 199 us -> 225 us
  starting transfers between devices: 237 us -> 256 us
    reduce_scatter x4, waiting for transfers between devices: 278 us -> 96.5 us  [on_device(): lax.psum_scatter(patch_back.astype(jnp.bfloat16), 'tile', scatter_dimensi...]
    all_gather x4 -> x0, waiting for transfers between devices: 56.4 us -> none  [on_device(): lax.all_gather(features.reshape(2 * height, 2 * width_dev * up_width), 't...]
    all_to_all x0 -> x3, waiting for transfers between devices: none -> 40.8 us  [on_device(): lax.all_to_all(jnp.stack([features.reshape(2 * height, 2 * width_dev * up...]
    all_to_all x0 -> x1, blocking collectives: none -> 28.4 us  [on_device(): lax.all_to_all(jnp.stack([features.reshape(2 * height, 2 * width_dev * up...]
    all_to_all x0 -> x3, starting transfers between devices: none -> 20.7 us  [on_device(): lax.all_to_all(jnp.stack([features.reshape(2 * height, 2 * width_dev * up...]
    another operation x18 -> x30, local copies, waits for them, and re-layouts: 0.2 us -> 20.6 us  [the longest x4 15.7 us: on_device(): gathered.reshape(2 * height // P_SIZE, P_SIZE, full_width // P_SIZE, P_SI...]
    unnamed x151 -> x147, local copies, waits for them, and re-layouts: 44.1 us -> 42.3 us
  transfers between devices with their start and end apart: 91 -> 90, of which waited for: 52 -> 50; matrix products, arithmetic and copies ran while one was open for 21% -> 23% of each run, Pallas kernels for 0% -> 0%
where the time goes in v1:
time: 1080 us; the launch traced here: 1070 us
  waiting for transfers between devices  339 us (31%)
  starting transfers between devices  256 us (24%)
  local copies, waits for them, and re-layouts  225 us (21%)
  matrix products  119 us (11%)
  other arithmetic  58 us (5%)
  blocking collectives  28.4 us (3%)
  loops' own time  24.6 us (2%)
  between operations  15 us (1%)
    reduce_scatter x4, waiting for transfers between devices, on_device(): lax.psum_scatter(patch_back.astype(jnp.bfloat16), 'tile', scatter_dimensi...  96.5 us
    ppermute x30, waiting for transfers between devices, with_halo(): lax.ppermute(tail, axis, [(i, (i + 1) % count) for i in range(ends)])  94.1 us
    ppermute x22, waiting for transfers between devices, from_behind(): return lax.ppermute(block, axis, route)  93.3 us
    ppermute x30, starting transfers between devices, with_halo(): lax.ppermute(head, axis, [((i + 1) % count, i) for i in range(ends)])  90.3 us
    ppermute x22, starting transfers between devices, from_behind(): return lax.ppermute(block, axis, route)  75.7 us
    ppermute x30, starting transfers between devices, with_halo(): lax.ppermute(tail, axis, [(i, (i + 1) % count) for i in range(ends)])  68.5 us
    convert_element_type x12, local copies, waits for them, and re-layouts, on_device(): patch_back.astype(jnp.bfloat16)  44.5 us
    unnamed x147, local copies, waits for them, and re-layouts  42.3 us
  transfers between devices with their start and end apart: 90, of which 50 were waited for; matrix products, arithmetic and copies ran while one was open for 23% of the time, Pallas kernels for 0%

profile of v1, /device:TPU:2, one launch (start us, length us, event | category | flops | bytes accessed | tf_op | source)
XLA Modules:
  0.0 1065.6 jit_solution(6767570335978162468)
XLA Ops:
  7.3 276.3 %while.49 = (s32[]{:T(128)}, bf16[8,6,384]{2,0,1:T(8,128)(2,1)S(1)}, bf16[8,6,384]{2,0,1:T(8,128)(2,1)S(1)}, bf16[8,4,384]{2,0,1:T(8,128)(2,1)S(1)}, bf16[4,8,4,...) while((s32[]{:T(128)}, ...), condition=%wide.region_5.6_spmd.clone, body=%wide.region_0.5_spmd.clone.sunk | while | flops 255259072 | bytes 13963990 | solution.py:133
  19.8 5.1 collective-permute-done.1
  25.0 5.1 conditional.6
  48.8 5.1 conditional.6
  75.5 5.1 conditional.6
  102.2 5.1 conditional.6
  129.7 9.3 collective-permute-start.2
  178.1 7.0 collective-permute-start.2
  224.2 7.1 collective-permute-start.2
  248.8 5.4 collective-permute-start.2
  271.6 10.5 collective-permute-start.2
  287.2 5.8 collective-permute-start.11
  296.0 5.8 collective-permute-start.7
  309.5 5.8 collective-permute-start.15
  319.9 5.9 collective-permute-start.19
  352.6 14.4 %all-gather.2.cloned.1.call-done = bf16[27,384,192]{2,0,1:T(8,128)(2,1)} async-done(((bf16[27,12,192]{2,0,1:T(8,128)(2,1)}), bf16[27,384,192]{2,0,1:T(8,128)(2,1)}) %all-gather.2.cloned.1.call-update) | async-done | bytes 3981328 | tf_op jit(solution)/shard_map/all_gather | solution.py:136
  367.0 10.1 multiply_convert_fusion.7
  378.5 6.0 all-to-all-start
  392.2 12.6 %all-to-all-done = bf16[32,16,1536]{2,1,0:T(8,128)(2,1)} async-done(((bf16[32,16,1536]{2,1,0:T(8,128)(2,1)}), bf16[32,16,1536]{2,1,0:T(8,128)(2,1)}, u32[]{:S(2)}, u32[]{:S(2)}) %all-to-all-start) | async-done | bytes 1572896 | tf_op jit(solution)/shard_map/all_to_all | solution.py:161
  420.2 7.7 convolution_convert_fusion.3
  440.5 9.4 multiply_convert_fusion.5
  451.4 7.4 all-to-all-start.1
  464.6 14.5 %all-to-all-done.1 = bf16[32,16,1536]{2,1,0:T(8,128)(2,1)} async-done(((bf16[32,16,1536]{2,1,0:T(8,128)(2,1)}), bf16[32,16,1536]{2,1,0:T(8,128)(2,1)}, u32[]{:S(2)}, u32[]{:S(2)}) %all-to-all-start.1) | async-done | bytes 1572896 | tf_op jit(solution)/shard_map/all_to_all | solution.py:161
  495.0 7.8 convolution_convert_fusion.2
  515.4 9.4 multiply_convert_fusion.3
  526.3 7.2 all-to-all-start.2
  540.0 13.7 %all-to-all-done.2 = bf16[32,16,1536]{2,1,0:T(8,128)(2,1)} async-done(((bf16[32,16,1536]{2,1,0:T(8,128)(2,1)}), bf16[32,16,1536]{2,1,0:T(8,128)(2,1)}, u32[]{:S(2)}, u32[]{:S(2)}) %all-to-all-start.2) | async-done | bytes 1572896 | tf_op jit(solution)/shard_map/all_to_all | solution.py:161
  566.1 7.3 convolution_convert_fusion.1
  583.4 9.5 multiply_convert_fusion.1
  593.2 28.4 %all_to_all.20 = bf16[32,16,1536]{2,1,0:T(8,128)(2,1)S(1)} all-to-all(bf16[32,16,1536]{2,1,0:T(8,128)(2,1)S(1)} %stack.270), channel_id=1, replica_groups=mesh['segment'=8,'tile'=32] {'tile'}, dimensions={0} | all-to-all | bytes 3145728 | tf_op jit(solution)/shard_map/all_to_all | solution.py:161
  632.3 7.3 convolution_convert_fusion
  649.4 11.5 %copy.651 = bf16[27,384,384]{2,1,0:T(8,128)(2,1)} copy(bf16[27,384,384]{1,2,0:T(8,128)(2,1)} %bitcast.1100) | data formatting | bytes 15925248 | tf_op jit(solution)/shard_map/transpose | solution.py:86
  661.0 8.7 copy.546
  669.7 5.5 copy.547
  677.9 6.5 copy.548
  688.0 5.0 collective-permute-start.9
  696.0 5.8 collective-permute-start.13
  701.8 8.3 reduce-scatter.9.cloned.1.call-done
  711.1 88.2 %reduce-scatter.11.cloned.1.call-done = bf16[16,1536]{1,0:T(8,128)(2,1)} async-done(((bf16[16,49152]{1,0:T(8,128)(2,1)}), bf16[16,1536]{1,0:T(8,128)(2,1)}) %reduce-scatter.11.cloned.1.call-update) | async-done | bytes 49168 | tf_op jit(solution)/shard_map/reduce_scatter | solution.py:188
  802.2 5.8 collective-permute-start.17
  811.4 6.0 collective-permute-start.21
  836.9 221.2 %while.50 = (s32[]{:T(128)}, bf16[8,6,384]{2,0,1:T(8,128)(2,1)S(1)}, bf16[8,6,384]{2,0,1:T(8,128)(2,1)S(1)}, f32[8,4,384]{2,0,1:T(8,128)S(1)}, f32[4,8,4,384]{3,...) while((s32[]{:T(128)}, ...), condition=%wide.region_20.21_spmd.clone, body=%wide.region_14.20_spmd.clone.sunk | while | flops 255418992 | bytes 14603769 | solution.py:251
  923.7 4.9 collective-permute-done.5
  939.9 33.6 %collective-permute-done.5 = bf16[8,4,384]{2,0,1:T(8,128)(2,1)S(1)} collective-permute-done((bf16[8,4,384]{2,0,1:T(8,128)(2,1)S(1)}, bf16[8,4,384]{2,0,1:T(8,128)(2,1)S(1)}, u32[]{:S(2)}, u32[]{:S(2)}) %collective-permute-start.5) | collective-permute-done | bytes 24608 | tf_op jit(solution)/shard_map/while/body/eval_jaxpr/ppermute | solution.py:30
  982.6 5.4 conditional.7
  1004.1 5.4 conditional.7
  1025.6 5.4 conditional.7
  1047.0 5.4 conditional.7
  (996 shorter events, 596.4 us)
Async XLA Ops:
  6.5 360.5 %all-gather.2.cloned.1.call-start = ((), (), s32[]{:S(2)}) async-start(), calls=%async_computation.8 | async-start | bytes 6488064 | tf_op jit(solution)/shard_map/all_gather | solution.py:136
  17.9 7.1 collective-permute-start.1
  41.7 7.1 collective-permute-start.1
  68.4 7.1 collective-permute-start.1
  95.1 7.1 collective-permute-start.1
  121.9 7.1 collective-permute-start.1
  129.7 10.8 %collective-permute-start.2 = (bf16[8,4,384]{2,0,1:T(8,128)(2,1)S(1)}, bf16[8,4,384]{2,0,1:T(8,128)(2,1)S(1)}, u32[]{:S(2)}, u32[]{:S(2)}) collective-permute-start(bf16[8,4,384]{2,0,1:T(8,128)(2,1)S(1)} %get-tuple-element.1160), channel_id=1, source_target_pairs={{0,32},{32,64},{64,96},{96,128},{128,160},{160,192},{192,224},{1,3... | collective-permute-start | bytes 73736 | tf_op jit(solution)/shard_map/while/body/eval_jaxpr/ppermute | solution.py:30
  148.6 7.1 collective-permute-start.1
  170.3 7.1 collective-permute-start.1
  178.1 8.5 collective-permute-start.2
  194.7 7.1 collective-permute-start.1
  216.4 7.1 collective-permute-start.1
  224.2 8.6 collective-permute-start.2
  240.9 7.1 collective-permute-start.1
  263.8 7.1 collective-permute-start.1
  271.6 12.0 %collective-permute-start.2 = (bf16[8,4,384]{2,0,1:T(8,128)(2,1)S(1)}, bf16[8,4,384]{2,0,1:T(8,128)(2,1)S(1)}, u32[]{:S(2)}, u32[]{:S(2)}) collective-permute-start(bf16[8,4,384]{2,0,1:T(8,128)(2,1)S(1)} %get-tuple-element.1160), channel_id=1, source_target_pairs={{0,32},{32,64},{64,96},{96,128},{128,160},{160,192},{192,224},{1,3... | collective-permute-start | bytes 73736 | tf_op jit(solution)/shard_map/while/body/eval_jaxpr/ppermute | solution.py:30
  285.3 24.2 %collective-permute-start.10 = (bf16[3,16,1,384]{3,2,1,0:T(2,128)(2,1)}, bf16[3,16,1,384]{3,2,1,0:T(2,128)(2,1)S(1)}, u32[]{:S(2)}, u32[]{:S(2)}) collective-permute-start(bf16[3,16,1,384]{3,2,1,0:T(2,128)(2,1)} %get-tuple-element.963), channel_id=1, source_target_pairs={{0,1},{1,2},{2,3},{3,4},{4,5},{5,6},{6,7},{7,8},{8,9},{9,10},{10,1... | collective-permute-start | bytes 110600 | tf_op jit(solution)/shard_map/ppermute | solution.py:18
  287.2 28.1 %collective-permute-start.11 = (bf16[3,16,1,384]{3,2,1,0:T(2,128)(2,1)}, bf16[3,16,1,384]{3,2,1,0:T(2,128)(2,1)}, u32[]{:S(2)}, u32[]{:S(2)}) collective-permute-start(bf16[3,16,1,384]{3,2,1,0:T(2,128)(2,1)} %get-tuple-element.964), channel_id=1, source_target_pairs={{1,0},{2,1},{3,2},{4,3},{5,4},{6,5},{7,6},{8,7},{9,8},{10,9},{11,1... | collective-permute-start | bytes 110600 | tf_op jit(solution)/shard_map/ppermute | solution.py:20
  294.1 25.9 %collective-permute-start.6 = (bf16[3,16,1,384]{3,2,1,0:T(2,128)(2,1)}, bf16[3,16,1,384]{3,2,1,0:T(2,128)(2,1)S(1)}, u32[]{:S(2)}, u32[]{:S(2)}) collective-permute-start(bf16[3,16,1,384]{3,2,1,0:T(2,128)(2,1)} %get-tuple-element.961), channel_id=1, source_target_pairs={{0,1},{1,2},{2,3},{3,4},{4,5},{5,6},{6,7},{7,8},{8,9},{9,10},{10,1... | collective-permute-start | bytes 110600 | tf_op jit(solution)/shard_map/ppermute | solution.py:18
  296.0 29.9 %collective-permute-start.7 = (bf16[3,16,1,384]{3,2,1,0:T(2,128)(2,1)}, bf16[3,16,1,384]{3,2,1,0:T(2,128)(2,1)}, u32[]{:S(2)}, u32[]{:S(2)}) collective-permute-start(bf16[3,16,1,384]{3,2,1,0:T(2,128)(2,1)} %get-tuple-element.962), channel_id=1, source_target_pairs={{1,0},{2,1},{3,2},{4,3},{5,4},{6,5},{7,6},{8,7},{9,8},{10,9},{11,1... | collective-permute-start | bytes 110600 | tf_op jit(solution)/shard_map/ppermute | solution.py:20
  307.5 21.5 %collective-permute-start.14 = (bf16[3,16,1,384]{3,2,1,0:T(2,128)(2,1)}, bf16[3,16,1,384]{3,2,1,0:T(2,128)(2,1)S(1)}, u32[]{:S(2)}, u32[]{:S(2)}) collective-permute-start(bf16[3,16,1,384]{3,2,1,0:T(2,128)(2,1)} %get-tuple-element.965), channel_id=1, source_target_pairs={{0,1},{1,2},{2,3},{3,4},{4,5},{5,6},{6,7},{7,8},{8,9},{9,10},{10,1... | collective-permute-start | bytes 110600 | tf_op jit(solution)/shard_map/ppermute | solution.py:18
  309.5 19.7 %collective-permute-start.15 = (bf16[3,16,1,384]{3,2,1,0:T(2,128)(2,1)}, bf16[3,16,1,384]{3,2,1,0:T(2,128)(2,1)S(1)}, u32[]{:S(2)}, u32[]{:S(2)}) collective-permute-start(bf16[3,16,1,384]{3,2,1,0:T(2,128)(2,1)} %get-tuple-element.966), channel_id=1, source_target_pairs={{1,0},{2,1},{3,2},{4,3},{5,4},{6,5},{7,6},{8,7},{9,8},{10,9},{11,1... | collective-permute-start | bytes 110600 | tf_op jit(solution)/shard_map/ppermute | solution.py:20
  318.0 24.5 %collective-permute-start.18 = (bf16[3,16,1,384]{3,2,1,0:T(2,128)(2,1)}, bf16[3,16,1,384]{3,2,1,0:T(2,128)(2,1)S(1)}, u32[]{:S(2)}, u32[]{:S(2)}) collective-permute-start(bf16[3,16,1,384]{3,2,1,0:T(2,128)(2,1)} %get-tuple-element.967), channel_id=1, source_target_pairs={{0,1},{1,2},{2,3},{3,4},{4,5},{5,6},{6,7},{7,8},{8,9},{9,10},{10,1... | collective-permute-start | bytes 110600 | tf_op jit(solution)/shard_map/ppermute | solution.py:18
  319.9 21.8 %collective-permute-start.19 = (bf16[3,16,1,384]{3,2,1,0:T(2,128)(2,1)}, bf16[3,16,1,384]{3,2,1,0:T(2,128)(2,1)S(1)}, u32[]{:S(2)}, u32[]{:S(2)}) collective-permute-start(bf16[3,16,1,384]{3,2,1,0:T(2,128)(2,1)} %get-tuple-element.968), channel_id=1, source_target_pairs={{1,0},{2,1},{3,2},{4,3},{5,4},{6,5},{7,6},{8,7},{9,8},{10,9},{11,1... | collective-permute-start | bytes 110600 | tf_op jit(solution)/shard_map/ppermute | solution.py:20
  378.5 26.2 %all-to-all-start = ((bf16[32,16,1536]{2,1,0:T(8,128)(2,1)}), bf16[32,16,1536]{2,1,0:T(8,128)(2,1)}, u32[]{:S(2)}, u32[]{:S(2)}) async-start(bf16[32,16,1536]{2,1,0:T(8,128)(2,1)} %stack.234), calls=%async_computation | async-start | bytes 3145728 | tf_op jit(solution)/shard_map/all_to_all | solution.py:161
  384.6 299.8 %reduce-scatter.5.cloned.1.call-start = ((), (), s32[]{:S(2)}) async-start(), calls=%async_computation.9 | async-start | bytes 1622016 | tf_op jit(solution)/shard_map/reduce_scatter | solution.py:188
  451.4 27.7 %all-to-all-start.1 = ((bf16[32,16,1536]{2,1,0:T(8,128)(2,1)}), bf16[32,16,1536]{2,1,0:T(8,128)(2,1)}, u32[]{:S(2)}, u32[]{:S(2)}) async-start(bf16[32,16,1536]{2,1,0:T(8,128)(2,1)} %stack.246), calls=%async_computation.2 | async-start | bytes 3145728 | tf_op jit(solution)/shard_map/all_to_all | solution.py:161
  458.8 234.3 %reduce-scatter.7.cloned.1.call-start = ((), (), s32[]{:S(2)}) async-start(), calls=%async_computation.10 | async-start | bytes 1622016 | tf_op jit(solution)/shard_map/reduce_scatter | solution.py:188
  526.3 27.5 %all-to-all-start.2 = ((bf16[32,16,1536]{2,1,0:T(8,128)(2,1)}), bf16[32,16,1536]{2,1,0:T(8,128)(2,1)}, u32[]{:S(2)}, u32[]{:S(2)}) async-start(bf16[32,16,1536]{2,1,0:T(8,128)(2,1)} %stack.258), calls=%async_computation.4 | async-start | bytes 3145728 | tf_op jit(solution)/shard_map/all_to_all | solution.py:161
  533.5 176.6 %reduce-scatter.9.cloned.1.call-start = ((), (), s32[]{:S(2)}) async-start(), calls=%async_computation.11 | async-start | bytes 1622016 | tf_op jit(solution)/shard_map/reduce_scatter | solution.py:188
  583.1 216.1 %reduce-scatter.11.cloned.1.call-start = ((), (), s32[]{:S(2)}) async-start(), calls=%async_computation.12 | async-start | bytes 1622016 | tf_op jit(solution)/shard_map/reduce_scatter | solution.py:188
  685.4 116.8 %collective-permute-start.8 = (bf16[16,1,192]{2,1,0:T(2,128)(2,1)S(1)}, bf16[16,1,192]{2,1,0:T(2,128)(2,1)S(1)}, u32[]{:S(2)}, u32[]{:S(2)}) collective-permute-start(bf16[16,1,192]{2,1,0:T(2,128)(2,1)S(1)} %get-tuple-element.985), channel_id=1, source_target_pairs={{0,1},{1,2},{2,3},{3,4},{4,5},{5,6},{6,7},{7,8},{8,9},{9,10},{10,1... | collective-permute-start | bytes 18440 | tf_op jit(solution)/shard_map/ppermute | solution.py:18
  688.0 119.9 %collective-permute-start.9 = (bf16[16,1,192]{2,1,0:T(2,128)(2,1)S(1)}, bf16[16,1,192]{2,1,0:T(2,128)(2,1)S(1)}, u32[]{:S(2)}, u32[]{:S(2)}) collective-permute-start(bf16[16,1,192]{2,1,0:T(2,128)(2,1)S(1)} %get-tuple-element.986), channel_id=1, source_target_pairs={{1,0},{2,1},{3,2},{4,3},{5,4},{6,5},{7,6},{8,7},{9,8},{10,9},{11,1... | collective-permute-start | bytes 18440 | tf_op jit(solution)/shard_map/ppermute | solution.py:20
  694.1 117.3 %collective-permute-start.12 = (bf16[16,1,192]{2,1,0:T(2,128)(2,1)S(1)}, bf16[16,1,192]{2,1,0:T(2,128)(2,1)S(1)}, u32[]{:S(2)}, u32[]{:S(2)}) collective-permute-start(bf16[16,1,192]{2,1,0:T(2,128)(2,1)S(1)} %get-tuple-element.987), channel_id=1, source_target_pairs={{0,1},{1,2},{2,3},{3,4},{4,5},{5,6},{6,7},{7,8},{8,9},{9,10},{10,1... | collective-permute-start | bytes 18440 | tf_op jit(solution)/shard_map/ppermute | solution.py:18
  696.0 121.4 %collective-permute-start.13 = (bf16[16,1,192]{2,1,0:T(2,128)(2,1)S(1)}, bf16[16,1,192]{2,1,0:T(2,128)(2,1)S(1)}, u32[]{:S(2)}, u32[]{:S(2)}) collective-permute-start(bf16[16,1,192]{2,1,0:T(2,128)(2,1)S(1)} %get-tuple-element.988), channel_id=1, source_target_pairs={{1,0},{2,1},{3,2},{4,3},{5,4},{6,5},{7,6},{8,7},{9,8},{10,9},{11,1... | collective-permute-start | bytes 18440 | tf_op jit(solution)/shard_map/ppermute | solution.py:20
  800.3 24.4 %collective-permute-start.16 = (bf16[16,1,192]{2,1,0:T(2,128)(2,1)S(1)}, bf16[16,1,192]{2,1,0:T(2,128)(2,1)S(1)}, u32[]{:S(2)}, u32[]{:S(2)}) collective-permute-start(bf16[16,1,192]{2,1,0:T(2,128)(2,1)S(1)} %get-tuple-element.989), channel_id=1, source_target_pairs={{0,1},{1,2},{2,3},{3,4},{4,5},{5,6},{6,7},{7,8},{8,9},{9,10},{10,1... | collective-permute-start | bytes 18440 | tf_op jit(solution)/shard_map/ppermute | solution.py:18
  802.2 22.4 %collective-permute-start.17 = (bf16[16,1,192]{2,1,0:T(2,128)(2,1)S(1)}, bf16[16,1,192]{2,1,0:T(2,128)(2,1)S(1)}, u32[]{:S(2)}, u32[]{:S(2)}) collective-permute-start(bf16[16,1,192]{2,1,0:T(2,128)(2,1)S(1)} %get-tuple-element.990), channel_id=1, source_target_pairs={{1,0},{2,1},{3,2},{4,3},{5,4},{6,5},{7,6},{8,7},{9,8},{10,9},{11,1... | collective-permute-start | bytes 18440 | tf_op jit(solution)/shard_map/ppermute | solution.py:20
  809.5 20.8 %collective-permute-start.20 = (bf16[16,1,192]{2,1,0:T(2,128)(2,1)S(1)}, bf16[16,1,192]{2,1,0:T(2,128)(2,1)S(1)}, u32[]{:S(2)}, u32[]{:S(2)}) collective-permute-start(bf16[16,1,192]{2,1,0:T(2,128)(2,1)S(1)} %get-tuple-element.991), channel_id=1, source_target_pairs={{0,1},{1,2},{2,3},{3,4},{4,5},{5,6},{6,7},{7,8},{8,9},{9,10},{10,1... | collective-permute-start | bytes 18440 | tf_op jit(solution)/shard_map/ppermute | solution.py:18
  811.4 18.9 %collective-permute-start.21 = (bf16[16,1,192]{2,1,0:T(2,128)(2,1)S(1)}, bf16[16,1,192]{2,1,0:T(2,128)(2,1)S(1)}, u32[]{:S(2)}, u32[]{:S(2)}) collective-permute-start(bf16[16,1,192]{2,1,0:T(2,128)(2,1)S(1)} %get-tuple-element.992), channel_id=1, source_target_pairs={{1,0},{2,1},{3,2},{4,3},{5,4},{6,5},{7,6},{8,7},{9,8},{10,9},{11,1... | collective-permute-start | bytes 18440 | tf_op jit(solution)/shard_map/ppermute | solution.py:20
  853.9 7.1 collective-permute-start.4
  868.8 7.1 collective-permute-start.4
  883.7 7.1 collective-permute-start.4
  898.6 7.1 collective-permute-start.4
  914.6 7.1 collective-permute-start.4
  930.7 7.1 collective-permute-start.4
  937.9 35.6 %collective-permute-start.5 = (bf16[8,4,384]{2,0,1:T(8,128)(2,1)S(1)}, bf16[8,4,384]{2,0,1:T(8,128)(2,1)S(1)}, u32[]{:S(2)}, u32[]{:S(2)}) collective-permute-start(bf16[8,4,384]{2,0,1:T(8,128)(2,1)S(1)} %add_convert_fusion.2), channel_id=1, source_target_pairs={{32,0},{64,32},{96,64},{128,96},{160,128},{192,160},{224,192},{33,... | collective-permute-start | bytes 73736 | tf_op jit(solution)/shard_map/while/body/eval_jaxpr/ppermute | solution.py:30
  975.5 7.1 collective-permute-start.4
  1039.9 7.1 collective-permute-start.4
  (58 other events, 294.8 us)
Sparse Core Ops, SparseCore 0:
  301.9 65.0 all-gather.1
  440.6 85.9 reduce-scatter.4
  530.4 89.1 reduce-scatter.6
  623.3 86.7 reduce-scatter.8
  713.8 85.4 reduce-scatter.10
